TPU v7x, 32 devices: a whole 2x2x4 slice. The times are simulated.
32 devices in a mesh: exp: 16 (over z, y, core), strip: 2 (over x).
Axes of the slice: x: 2, y: 2, z: 4, core: 2. Of those that a mesh axis runs over, the one named last changes fastest.
Arguments:
- model: float32 [512, 2048], P('strip', 'exp'), may hold values from -6 to 6
- images: bfloat16 [16, 512, 2048], P('exp', 'strip'), may hold values from -6 to 6
- footprint: int32 [16, 4], replicated, may hold values from 0 to 2048, as said below
- psf_index: int32 [16], replicated, may hold values from 0 to 7, as said below
- exposure_weight: float32 [16], replicated, may hold values from 0.05 to 0.5
- psf_rows: bfloat16 [8, 4, 25], replicated, may hold values from -1.1953125 to 1.1953125
- psf_cols: bfloat16 [8, 4, 25], replicated, may hold values from -1.1953125 to 1.1953125
Outputs:
- new_model: float32 [512, 2048], P('strip', 'exp')
Inputs may be any that keep to these rules, and one draw needn't show every extreme that they name: `footprint`: each exposure spans 128 or more rows and 512 or more columns; one exposure spans the whole sky. `psf_index`: every PSF model is used by the same number of exposures.
All inputs are finite; a program needn't handle non-finite values.
Results may differ from a plain program's by a relative error of at most 0.005.
Values may be sent and summed in bfloat16 or wider, within the bound.
A program may use at most 128 MiB of HBM per device.

v0:
```python
import jax
import jax.numpy as jnp
from jax import lax
from jax.sharding import PartitionSpec as P

RANK = 4
TAPS = 25


step_size = 0.25
highest = lax.Precision.HIGHEST


def with_halo(cells, sides, width):
    for axis, dim in sides:
        count = lax.axis_size(axis)
        ends = count - 1
        head = lax.slice_in_dim(cells, 0, width, axis=dim)
        tail = lax.slice_in_dim(cells, cells.shape[dim] - width, cells.shape[dim], axis=dim)
        cells = jnp.concatenate(
            [
                lax.ppermute(tail, axis, [(i, (i + 1) % count) for i in range(ends)]),
                cells,
                lax.ppermute(head, axis, [((i + 1) % count, i) for i in range(ends)]),
            ],
            axis=dim,
        )
    return cells


def banded(tap_values, size_in, size_out, offset_lead, flipped):
    inner_index = jnp.arange(size_in, dtype=jnp.int32)[:, None]
    outer_index = jnp.arange(size_out, dtype=jnp.int32)[None, :]
    if flipped:
        offset = outer_index - inner_index + offset_lead
    else:
        offset = inner_index - outer_index - offset_lead
    onehot_table = (offset[None] == jnp.arange(TAPS, dtype=jnp.int32)[:, None, None]).astype(
        jnp.float32
    )
    return jnp.einsum("...t,tio->...io", tap_values, onehot_table, precision=highest).astype(
        jnp.bfloat16
    )


def shift_blocks(values, downward):
    zero_block = jnp.zeros_like(values[..., :1, :])
    if downward:
        return jnp.concatenate([zero_block, values[..., :-1, :]], axis=-2)
    return jnp.concatenate([values[..., 1:, :], zero_block], axis=-2)


def windows(values):
    return jnp.concatenate(
        [shift_blocks(values, True), values, shift_blocks(values, False)], axis=-1
    )


def fold_rims(rimmed, rows_here, half_taps):
    center = rimmed[2 * half_taps : 2 * half_taps + rows_here]
    upper = jnp.pad(rimmed[:half_taps], ((0, rows_here - half_taps), (0, 0)))
    lower = jnp.pad(rimmed[rows_here + 3 * half_taps :], ((rows_here - half_taps, 0), (0, 0)))
    return center + upper + lower


def local(model, images, footprint, psf_index, exposure_weight, psf_rows, psf_cols):
    half_taps = TAPS // 2
    column_block = 128
    rows_here = model.shape[0]
    strip_index = lax.axis_index("strip")
    column_index = lax.axis_index("exp")
    model_half = model.astype(jnp.bfloat16)
    select = (psf_index[:, None] == jnp.arange(psf_rows.shape[0], dtype=jnp.int32)[None, :]).astype(
        jnp.float32
    )
    all_rows = jnp.einsum("eb,bkt->ekt", select, psf_rows.astype(jnp.float32), precision=highest)
    all_cols = jnp.einsum("eb,bkt->ekt", select, psf_cols.astype(jnp.float32), precision=highest)
    rows_global = strip_index * rows_here + jnp.arange(rows_here, dtype=jnp.int32)
    picked = jnp.arange(psf_index.shape[0], dtype=jnp.int32) == column_index
    own_rows = jnp.einsum("e,ekt->kt", picked.astype(jnp.float32), all_rows, precision=highest)
    own_cols = jnp.einsum("e,ekt->kt", picked.astype(jnp.float32), all_cols, precision=highest)
    bounds = jnp.sum(jnp.where(picked[:, None], footprint, 0), axis=0)
    weight = jnp.sum(jnp.where(picked, exposure_weight, 0.0))
    exposure_image = images[0]
    width_all = exposure_image.shape[1]
    nblocks = width_all // column_block
    forward_rows = banded(own_rows, rows_here + 2 * half_taps, rows_here, 0, False)
    lift_rows = forward_rows.transpose(0, 2, 1).reshape(RANK * rows_here, rows_here + 2 * half_taps)
    drop_rows = forward_rows.transpose(1, 0, 2).reshape(rows_here + 2 * half_taps, RANK * rows_here)
    whole_strip = lax.all_gather(model_half, "exp", axis=1, tiled=True)
    edged_strip = with_halo(whole_strip, (("strip", 0),), half_taps)
    row_pass = jnp.dot(lift_rows, edged_strip, preferred_element_type=jnp.float32).astype(
        jnp.bfloat16
    )
    blocks = row_pass.reshape(RANK, rows_here, nblocks, column_block)
    segments = []
    for segment in range(3):
        band_piece = banded(
            own_cols,
            column_block,
            column_block,
            column_block - half_taps - segment * column_block,
            False,
        )
        segments.append(
            jnp.einsum("ksbw,kwo->sbo", blocks, band_piece, preferred_element_type=jnp.float32)
        )
    predicted = (
        shift_blocks(segments[0], True) + segments[1] + shift_blocks(segments[2], False)
    ).reshape(rows_here, width_all)
    cols_global = jnp.arange(width_all, dtype=jnp.int32)
    row_inside = (rows_global >= bounds[0]) & (rows_global < bounds[1])
    col_inside = (cols_global >= bounds[2]) & (cols_global < bounds[3])
    inside = row_inside[:, None] & col_inside[None, :]
    residual = jnp.where(
        inside, weight * (predicted - exposure_image.astype(jnp.float32)), 0.0
    ).astype(jnp.bfloat16)
    back_band = jnp.concatenate(
        [
            banded(
                own_cols,
                column_block,
                column_block,
                column_block + half_taps - segment * column_block,
                True,
            )
            for segment in range(3)
        ],
        axis=1,
    )
    adjoint = jnp.einsum(
        "sbw,kwo->ksbo",
        windows(residual.reshape(rows_here, nblocks, column_block)),
        back_band,
        preferred_element_type=jnp.float32,
    )
    adjoint = adjoint.astype(jnp.bfloat16).reshape(RANK * rows_here, width_all)
    spread = jnp.dot(drop_rows, adjoint, preferred_element_type=jnp.float32)
    rimmed = with_halo(spread, (("strip", 0),), half_taps)
    folded = fold_rims(rimmed, rows_here, half_taps)
    gradient = lax.psum_scatter(folded, "exp", scatter_dimension=1, tiled=True)
    return model - step_size * gradient


def solution(mesh):
    placed = (P("strip", "exp"), P("exp", "strip", None), P(), P(), P(), P(), P())
    return jax.shard_map(
        local, mesh=mesh, in_specs=placed, out_specs=P("strip", "exp"), check_vma=False
    )
```

profile of v0, /device:TPU:0, one launch (start us, length us, event | category | flops | bytes accessed | tf_op | source)
XLA Modules:
  0.0 176.1 jit_solution(6456711165828360169)
XLA Ops:
  6.5 1.6 convert_element_type.74
  18.0 1.6 fusion.42
  19.6 1.6 fusion.40
  21.2 1.6 fusion.38
  22.7 2.9 %fusion.53 = bf16[4,280,256]{2,0,1:T(4,128)(2,1)S(1)} fusion(f32[4,25,1]{1,0,2:T(4,128)S(1)} %bitcast.97, s32[280,256]{1,0:T(8,128)S(1)} %iota_subtract_fusion), kind=kOutput, calls=%fused_computation.56 | convolution fusion | flops 88094720 | bytes 860560 | tf_op jit(solution)/shard_map/...t,tio->...io/dot_general | solution.py:41
  25.6 23.3 %all-gather.2.cloned.1.call-done = bf16[256,2048]{1,0:T(8,128)(2,1)} async-done(((bf16[256,128]{1,0:T(8,128)(2,1)}), bf16[256,2048]{1,0:T(8,128)(2,1)}) %all-gather.2.cloned.1.call-update) | async-done | bytes 1048592 | tf_op jit(solution)/shard_map/all_gather | solution.py:90
  48.9 1.5 fusion.98
  50.4 4.0 %collective-permute-start = (bf16[12,2048]{1,0:T(8,128)(2,1)}, bf16[12,2048]{1,0:T(8,128)(2,1)}, u32[]{:S(2)}, u32[]{:S(2)}) collective-permute-start(bf16[12,2048]{1,0:T(8,128)(2,1)} %get-tuple-element.9), channel_id=1, source_target_pairs={{0,1},{2,3},{4,5},{6,7},{8,9},{10,11},{12,13},{14,15},{16,17},{18,... | collective-permute-start | bytes 147464 | tf_op jit(solution)/shard_map/ppermute | solution.py:22
  54.4 1.5 collective-permute-start.1
  60.4 1.7 copy.30
  62.1 1.7 copy.32
  63.8 3.8 %convert_bitcast_fusion.1 = bf16[128,8,16,128]{3,1,2,0:T(8,128)(2,1)S(1)} fusion(bf16[1024,280]{0,1:T(8,128)(2,1)} %bitcast.94, bf16[12,2048]{1,0:T(8,128)(2,1)} %collective-permute-done.1, bf16[256,2048]{1,0:T(8,128)(2,1)} %all-gather.2.cloned.1.call-done, bf16[12,2048]{1,0:T(8,128)(2,1)} %collective-permute-done), kind=kOutput, calls=%fused_computation.11 | convolution fusion | flops 1179942912 | bytes 5914624 | tf_op jit(solution)/shard_map/dot_general | solution.py:92
  69.1 1.5 fusion.44
  71.5 1.5 fusion.49
  73.2 3.9 %fusion.31 = bf16[256,16,128]{0,2,1:T(8,128)(2,1)S(1)} fusion(f32[256,16,128]{0,2,1:T(8,128)S(1)} %bitcast.92, f32[256,15,128]{0,2,1:T(8,128)S(1)} %slice.55, f32[256,15,128]{0,2,1:T(8,128)S(1)} %slice.54, bf16[4,256,16,128]{3,2,1,0:T(8,128)(2,1)S(1)} %bitcast.91, f32[]{:T(128)} %select_reduce_fusion.1, pred[16,128]{1,0:T(8,128)(4,1)S(1)} %fusion.81, ...), kind=kOutput, calls=%fused_computation.34 | convolution fusion | flops 540540928 | bytes 11405572 | tf_op jit(solution)/shard_map/ksbw,kwo->sbo/dot_general | solution.py:106
  78.1 3.8 %convert_bitcast_fusion = bf16[4,256,16,128]{1,3,2,0:T(8,128)(2,1)} fusion(bf16[256,15,128]{0,2,1:T(8,128)(2,1)S(1)} %get-tuple-element.8, bf16[256,15,128]{0,2,1:T(8,128)(2,1)S(1)} %get-tuple-element.7, bf16[256,16,128]{0,2,1:T(8,128)(2,1)S(1)} %fusion.31, bf16[4,128,128]{1,2,0:T(8,128)(2,1)S(1)} %copy-done.6, bf16[4,128,128]{1,2,0:T(8,128)(2,1)S(1)} %copy-done.5, ...), kind=kOutput, calls=%fused_computation.10 | convolution fusion | flops 1629618176 | bytes 7602176 | tf_op jit(solution)/shard_map/sbw,kwo->ksbo/dot_general | solution.py:131
  82.0 7.9 %copy.18 = bf16[4,256,16,128]{3,2,1,0:T(8,128)(2,1)} copy(bf16[4,256,16,128]{1,3,2,0:T(8,128)(2,1)} %convert_bitcast_fusion) | data formatting | bytes 8388608 | tf_op jit(solution)/shard_map/convert_element_type | solution.py:137
  89.8 3.6 %fusion.4 = f32[280,2048]{1,0:T(8,128)S(1)} fusion(bf16[280,1024]{1,0:T(8,128)(2,1)S(1)} %bitcast.95, bf16[128,8,16,128]{3,2,1,0:T(8,128)(2,1)} %bitcast.93), kind=kOutput, calls=%fused_computation.7 | convolution fusion | flops 1174405120 | bytes 7061504 | tf_op jit(solution)/shard_map/dot_general | solution.py:138
  93.5 5.0 %collective-permute-start.2 = (f32[12,2048]{1,0:T(8,128)S(1)}, f32[12,2048]{1,0:T(8,128)S(1)}, u32[]{:S(2)}, u32[]{:S(2)}) collective-permute-start(f32[12,2048]{1,0:T(8,128)S(1)} %get-tuple-element.5), channel_id=1, source_target_pairs={{0,1},{2,3},{4,5},{6,7},{8,9},{10,11},{12,13},{14,15},{16,17},{18,... | collective-permute-start | bytes 294920 | tf_op jit(solution)/shard_map/ppermute | solution.py:22
  98.5 1.4 collective-permute-start.3
  101.0 4.4 %collective-permute-done.3 = f32[12,2048]{1,0:T(8,128)S(1)} collective-permute-done((f32[12,2048]{1,0:T(8,128)S(1)}, f32[12,2048]{1,0:T(8,128)S(1)}, u32[]{:S(2)}, u32[]{:S(2)}) %collective-permute-start.3) | collective-permute-done | bytes 98336 | tf_op jit(solution)/shard_map/ppermute | solution.py:24
  105.5 1.6 fusion.26
  107.1 60.6 %reduce-scatter.2.cloned.1.call-done = f32[256,128]{1,0:T(8,128)} async-done(((f32[256,2048]{1,0:T(8,128)}), f32[256,128]{1,0:T(8,128)}) %reduce-scatter.2.cloned.1.call-update) | async-done | bytes 131088 | tf_op jit(solution)/shard_map/reduce_scatter | solution.py:141
  167.7 1.6 multiply_subtract_fusion
  (64 shorter events, 18.9 us)
Async XLA Ops:
  6.5 1.8 %copy-start = (bf16[8,4,25]{2,1,0:T(4,128)(2,1)S(1)}, bf16[8,4,25]{2,1,0:T(4,128)(2,1)}, u32[]{:S(2)}) copy-start(bf16[8,4,25]{2,1,0:T(4,128)(2,1)} %param.12) | copy-start | bytes 4804
  6.5 6.0 %copy-start.9 = (f32[16]{0:T(128)S(1)}, f32[16]{0:T(128)}, u32[]{:S(2)}) copy-start(f32[16]{0:T(128)} %param.11) | copy-start | bytes 196
  6.5 42.4 %all-gather.2.cloned.1.call-start = ((), (), s32[]{:S(2)}) async-start(), calls=%async_computation.1 | async-start | bytes 1114112 | tf_op jit(solution)/shard_map/all_gather | solution.py:90
  8.1 159.6 %reduce-scatter.2.cloned.1.call-start = ((), (), s32[]{:S(2)}) async-start(), calls=%async_computation.2 | async-start | bytes 2228224 | tf_op jit(solution)/shard_map/reduce_scatter | solution.py:141
  22.7 37.0 %copy-start.1 = (bf16[1,256,2048]{2,1,0:T(8,128)(2,1)S(1)}, bf16[1,256,2048]{2,1,0:T(8,128)(2,1)}, u32[]{:S(2)}) copy-start(bf16[1,256,2048]{2,1,0:T(8,128)(2,1)} %param.8) | copy-start | bytes 3145732
  50.4 13.4 %collective-permute-start = (bf16[12,2048]{1,0:T(8,128)(2,1)}, bf16[12,2048]{1,0:T(8,128)(2,1)}, u32[]{:S(2)}, u32[]{:S(2)}) collective-permute-start(bf16[12,2048]{1,0:T(8,128)(2,1)} %get-tuple-element.9), channel_id=1, source_target_pairs={{0,1},{2,3},{4,5},{6,7},{8,9},{10,11},{12,13},{14,15},{16,17},{18,... | collective-permute-start | bytes 147464 | tf_op jit(solution)/shard_map/ppermute | solution.py:22
  54.4 9.4 %collective-permute-start.1 = (bf16[12,2048]{1,0:T(8,128)(2,1)S(1)}, bf16[12,2048]{1,0:T(8,128)(2,1)}, u32[]{:S(2)}, u32[]{:S(2)}) collective-permute-start(bf16[12,2048]{1,0:T(8,128)(2,1)S(1)} %get-tuple-element.10), channel_id=1, source_target_pairs={{1,0},{3,2},{5,4},{7,6},{9,8},{11,10},{13,12},{15,14},{17,16},{19,... | collective-permute-start | bytes 147464 | tf_op jit(solution)/shard_map/ppermute | solution.py:24
  57.1 3.2 %copy-start.4 = (bf16[4,128,128]{2,0,1:T(4,128)(2,1)S(1)}, bf16[4,128,128]{2,0,1:T(4,128)(2,1)}, u32[]{:S(2)}) copy-start(bf16[4,128,128]{2,0,1:T(4,128)(2,1)} %fusion.42) | copy-start | bytes 393220
  67.6 1.4 copy-start.8
  70.6 0.9 copy-start.7
  77.2 0.9 copy-start.5
  77.2 1.0 copy-start.6
  81.9 7.9 %copy-start.2 = (bf16[35,8,4,256]{3,1,2,0:T(8,128)(2,1)S(1)}, bf16[35,8,4,256]{3,1,2,0:T(8,128)(2,1)}, u32[]{:S(2)}) copy-start(bf16[35,8,4,256]{3,1,2,0:T(8,128)(2,1)} %copy.45) | copy-start | bytes 1720324
  93.5 7.6 %collective-permute-start.2 = (f32[12,2048]{1,0:T(8,128)S(1)}, f32[12,2048]{1,0:T(8,128)S(1)}, u32[]{:S(2)}, u32[]{:S(2)}) collective-permute-start(f32[12,2048]{1,0:T(8,128)S(1)} %get-tuple-element.5), channel_id=1, source_target_pairs={{0,1},{2,3},{4,5},{6,7},{8,9},{10,11},{12,13},{14,15},{16,17},{18,... | collective-permute-start | bytes 294920 | tf_op jit(solution)/shard_map/ppermute | solution.py:22
  98.5 69.2 %copy-start.3 = (f32[256,128]{1,0:T(8,128)S(1)}, f32[256,128]{1,0:T(8,128)}, u32[]{:S(2)}) copy-start(f32[256,128]{1,0:T(8,128)} %param.7) | copy-start | bytes 393220
  98.5 7.0 %collective-permute-start.3 = (f32[12,2048]{1,0:T(8,128)S(1)}, f32[12,2048]{1,0:T(8,128)S(1)}, u32[]{:S(2)}, u32[]{:S(2)}) collective-permute-start(f32[12,2048]{1,0:T(8,128)S(1)} %get-tuple-element.6), channel_id=1, source_target_pairs={{1,0},{3,2},{5,4},{7,6},{9,8},{11,10},{13,12},{15,14},{17,16},{19,... | collective-permute-start | bytes 294920 | tf_op jit(solution)/shard_map/ppermute | solution.py:24
Sparse Core Ops, SparseCore 0:
  9.5 39.3 all-gather.1
  107.2 60.4 reduce-scatter.1
where the time goes:
time: 177 us; the launch traced here: 176 us
  waiting for transfers between devices  89.5 us (51%)
  matrix products  30.6 us (17%)
  local copies, waits for them, and re-layouts  20.2 us (11%)
  between operations  13.8 us (8%)
  starting transfers between devices  11.9 us (7%)
  other arithmetic  10.2 us (6%)
    reduce_scatter x1, waiting for transfers between devices, local(): gradient = lax.psum_scatter(folded, 'exp', scatter_dimension=1, tiled=True)  60.6 us
    all_gather x1, waiting for transfers between devices, local(): whole_strip = lax.all_gather(model_half, 'exp', axis=1, tiled=True)  23.3 us
    dot_general x7, matrix products, banded(): jnp.einsum('...t,tio->...io', tap_values, onehot_table, precision=highest)  10.4 us
    ppermute x2, starting transfers between devices, with_halo(): lax.ppermute(tail, axis, [(i, (i + 1) % count) for i in range(ends)])  8.96 us
    convert_element_type x1, local copies, waits for them, and re-layouts, local(): adjoint = adjoint.astype(jnp.bfloat16).reshape(RANK * rows_here, width_all)  7.89 us
    dot_general x3, matrix products, local(): jnp.einsum('ksbw,kwo->sbo', blocks, band_piece, preferred_element_type=jn...  6.97 us
    dot_general x6, local copies, waits for them, and re-layouts, banded(): jnp.einsum('...t,tio->...io', tap_values, onehot_table, precision=highest)  5.16 us
    ppermute x2, waiting for transfers between devices, with_halo(): lax.ppermute(head, axis, [((i + 1) % count, i) for i in range(ends)])  4.43 us
  transfers between devices with their start and end apart: 6, of which 4 were waited for; matrix products, arithmetic and copies ran while one was open for 14% of the time, Pallas kernels for 0%

commit v1 on v0

v1 whole, which is shorter than its diff:
```python
import functools

import jax
import jax.numpy as jnp
from jax import lax
from jax.experimental import pallas as pl
from jax.experimental.pallas import tpu as pltpu
from jax.sharding import PartitionSpec as P

RANK = 4
TAPS = 25
HALF = TAPS // 2
RIM = 16
LANES = 128
step_size = 0.25
MESH = pl.DeviceIdType.MESH
VMEM = pl.BlockSpec(memory_space=pltpu.VMEM)
SMEM = pl.BlockSpec(memory_space=pltpu.SMEM)


def places(n):
    line = n // 4
    if line < 8:
        split = lambda i: (i // 4, (i // 2) % 2, i % 2)
        join = lambda l, p, c: l * 4 + p * 2 + c
    else:
        split = lambda i: ((i // 2) % line, i // (2 * line), i % 2)
        join = lambda l, p, c: p * (2 * line) + l * 2 + c
    return line, split, join


def greet(devices):
    barrier = pltpu.get_barrier_semaphore()
    for device in devices:
        pl.semaphore_signal(barrier, inc=1, device_id=device, device_id_type=MESH)
    pl.semaphore_wait(barrier, len(devices))


def gather_kernel(n, strips, model_ref, x_ref, halo_send, halo_recv, line_send, line_recv,
                  pair_send, pair_recv, core_send, core_recv):
    line, split, join = places(n)
    me = lax.axis_index("exp")
    strip = lax.axis_index("strip")
    l, p, c = split(me)
    rows = model_ref.shape[0]
    above = {"strip": (strip + strips - 1) % strips}
    below = {"strip": (strip + 1) % strips}
    peers = [{"exp": join((l + q) % line, p, c)} for q in range(line)]
    pair = {"exp": join(l, 1 - p, c)}
    core = {"exp": join(l, p, 1 - c)}

    def push(src, dst, send, recv, device):
        copy = pltpu.make_async_remote_copy(
            src_ref=src, dst_ref=dst, send_sem=send, recv_sem=recv, device_id=device,
            device_id_type=MESH,
        )
        copy.start()
        return copy

    x_ref[me, RIM : RIM + rows, :] = model_ref[...].astype(jnp.bfloat16)
    greet([above, below, pair, core] + peers[1:])
    halos = [
        push(x_ref.at[me, pl.ds(RIM, RIM)], x_ref.at[me, pl.ds(RIM + rows, RIM)],
             halo_send.at[0], halo_recv.at[0], above),
        push(x_ref.at[me, pl.ds(rows, RIM)], x_ref.at[me, pl.ds(0, RIM)],
             halo_send.at[1], halo_recv.at[1], below),
    ]
    for copy in halos:
        copy.wait()
    order = [0]
    for q in range(1, line // 2 + 1):
        order += [q, line - q] if q != line - q else [q]
    along = {}
    for q in reversed(order[1:]):
        along[q] = push(x_ref.at[me], x_ref.at[me], line_send.at[q], line_recv.at[q], peers[q])
    over, across = [], []
    for q in order:
        slot = join((l + line - q) % line, p, c)
        if q:
            along[q].wait_recv()
        over.append(
            push(x_ref.at[slot], x_ref.at[slot], pair_send.at[q], pair_recv.at[q], pair)
        )
        across.append(
            push(x_ref.at[slot], x_ref.at[slot], core_send.at[q], core_recv.at[q], core)
        )
    for place, q in enumerate(order):
        slot = join((l + line - q) % line, 1 - p, c)
        over[place].wait_recv()
        across.append(
            push(x_ref.at[slot], x_ref.at[slot], core_send.at[line + q], core_recv.at[line + q],
                 core)
        )
    for copy in across:
        copy.wait()
    for copy in over:
        copy.wait_send()
    for q in order[1:]:
        along[q].wait_send()


def gather(n, strips, model):
    line = n // 4
    rows = model.shape[0]
    dma = pltpu.SemaphoreType.DMA
    return pl.pallas_call(
        functools.partial(gather_kernel, n, strips),
        out_shape=jax.ShapeDtypeStruct((n, rows + 2 * RIM, LANES), jnp.bfloat16),
        in_specs=[VMEM],
        out_specs=VMEM,
        scratch_shapes=[dma((2,)), dma((2,)), dma((line,)), dma((line,)), dma((line,)),
                        dma((line,)), dma((2 * line,)), dma((2 * line,))],
        compiler_params=pltpu.CompilerParams(collective_id=0, has_side_effects=True),
    )(model)


def compute_kernel(n, strips, rows_part, footprint, psf_index, weights, psf_rows, psf_cols, image,
                   x_ref, g_ref, lift, drop, fore, back, rp, res):
    f32, bf16 = jnp.float32, jnp.bfloat16
    me = lax.axis_index("exp")
    strip = lax.axis_index("strip")
    rows = image.shape[0]
    wide = n * LANES
    chosen = psf_index[me]

    def taps_of(table):
        total = jnp.zeros((RANK, TAPS), f32)
        for b in range(table.shape[0]):
            total = total + jnp.where(chosen == b, table[b].astype(f32), 0.0)
        return total.astype(bf16)

    tap = lax.broadcasted_iota(jnp.int32, (TAPS, 384), 0)
    lane = lax.broadcasted_iota(jnp.int32, (TAPS, 384), 1)
    same = (tap == lane).astype(f32).astype(bf16)
    mirror = (tap + lane == TAPS - 1).astype(f32).astype(bf16)
    row_taps = jnp.dot(taps_of(psf_rows), same, preferred_element_type=f32)
    col_taps = taps_of(psf_cols)
    col_fore = jnp.dot(col_taps, mirror, preferred_element_type=f32)
    col_back = jnp.dot(col_taps, same, preferred_element_type=f32)

    def slanted(vector, width, shift):
        spread = jnp.broadcast_to(vector[:, :width], (LANES, width))
        return pltpu.roll(pltpu.roll(spread, 0, 1, stride=1, stride_axis=0), shift, 1)

    fore[...] = jnp.zeros_like(fore)
    back[...] = jnp.zeros_like(back)
    for k in range(RANK):
        band = slanted(row_taps[k : k + 1], 256, RIM - HALF)
        lift[k * LANES : (k + 1) * LANES, :] = band[:, : LANES + 2 * RIM].astype(bf16)
        drop[:, k * LANES : (k + 1) * LANES] = band.T[: LANES + 2 * RIM].astype(bf16)
        for ref, vectors in ((fore, col_fore), (back, col_back)):
            strip_band = slanted(vectors[k : k + 1], 384, LANES - HALF).astype(bf16)
            for o in range(2):
                for d in range(3):
                    ref[k, (o + d) * LANES : (o + d + 1) * LANES, o * LANES : (o + 1) * LANES] = (
                        strip_band[:, (2 - d) * LANES : (3 - d) * LANES]
                    )

    edge = jnp.zeros((rows, LANES), bf16)
    for k in range(RANK):
        rp[k, :, :LANES] = edge
        rp[k, :, wide + LANES :] = edge
    res[:, :LANES] = edge
    res[:, wide + LANES :] = edge

    top = jnp.where(strip > 0, 1.0, 0.0)
    bottom = jnp.where(strip < strips - 1, 1.0, 0.0)
    parts = rows // LANES
    window = LANES + 2 * RIM

    def row_step(b, carry):
        left = x_ref[2 * b]
        right = x_ref[2 * b + 1]
        cells = jnp.concatenate([left, right], axis=1)
        upper = (cells[:RIM].astype(f32) * top).astype(bf16)
        lower = (cells[rows + RIM :].astype(f32) * bottom).astype(bf16)
        cells = jnp.concatenate([upper, cells[RIM : rows + RIM], lower], axis=0)
        at = pl.ds(pl.multiple_of(256 * b + LANES, LANES), 256)
        for s in range(parts):
            out = jnp.dot(lift[...], cells[s * LANES : s * LANES + window],
                          preferred_element_type=f32).astype(bf16)
            for k in range(RANK):
                rp[k, s * LANES : (s + 1) * LANES, at] = out[k * LANES : (k + 1) * LANES]
        return carry

    lax.fori_loop(0, n // 2, row_step, 0)

    weight = weights[me]
    row_at = lax.broadcasted_iota(jnp.int32, (rows, 256), 0) + strip * rows
    col_at = lax.broadcasted_iota(jnp.int32, (rows, 256), 1)
    row_ok = (row_at >= footprint[me, 0]) & (row_at < footprint[me, 1])
    start, stop = footprint[me, 2], footprint[me, 3]

    def fore_step(b, carry):
        begin = pl.multiple_of(256 * b, 256)
        predicted = jnp.zeros((rows, 256), f32)
        for k in range(RANK):
            predicted = predicted + jnp.dot(rp[k, :, pl.ds(begin, 512)], fore[k],
                                            preferred_element_type=f32)
        inside = row_ok & (col_at >= start - 256 * b) & (col_at < stop - 256 * b)
        value = weight * (predicted - image[:, pl.ds(begin, 256)].astype(f32))
        res[:, pl.ds(pl.multiple_of(256 * b + LANES, LANES), 256)] = jnp.where(
            inside, value, 0.0
        ).astype(bf16)
        return carry

    lax.fori_loop(0, n // 2, fore_step, 0)

    def back_step(b, carry):
        cells = res[:, pl.ds(pl.multiple_of(256 * b, 256), 512)]
        spread = [
            jnp.dot(cells, back[k], preferred_element_type=f32).astype(bf16) for k in range(RANK)
        ]
        total = jnp.zeros((rows + 2 * RIM, 256), f32)
        pieces = []
        for s in range(parts):
            stack = jnp.concatenate([v[s * LANES : (s + 1) * LANES] for v in spread], axis=0)
            pieces.append(jnp.dot(drop[...], stack, preferred_element_type=f32))
        joined = [pieces[0][:LANES]]
        for s in range(1, parts):
            joined.append(pieces[s - 1][LANES:] + pieces[s][: 2 * RIM])
            joined.append(pieces[s][2 * RIM : LANES])
        joined.append(pieces[-1][LANES:])
        total = jnp.concatenate(joined, axis=0).astype(bf16)
        g_ref[2 * b] = total[:, :LANES]
        g_ref[2 * b + 1] = total[:, LANES:]
        return carry

    lax.fori_loop(0, n // 2, back_step, 0)


def compute(n, strips, footprint, psf_index, weights, psf_rows, psf_cols, image, x):
    rows = image.shape[0]
    bf16 = jnp.bfloat16
    window = LANES + 2 * RIM
    return pl.pallas_call(
        functools.partial(compute_kernel, n, strips, rows),
        out_shape=jax.ShapeDtypeStruct(x.shape, bf16),
        in_specs=[SMEM, SMEM, SMEM, VMEM, VMEM, VMEM, VMEM],
        out_specs=VMEM,
        scratch_shapes=[
            pltpu.VMEM((RANK * LANES, window), bf16),
            pltpu.VMEM((window, RANK * LANES), bf16),
            pltpu.VMEM((RANK, 4 * LANES, 2 * LANES), bf16),
            pltpu.VMEM((RANK, 4 * LANES, 2 * LANES), bf16),
            pltpu.VMEM((RANK, rows, (n + 2) * LANES), bf16),
            pltpu.VMEM((rows, (n + 2) * LANES), bf16),
        ],
    )(footprint, psf_index, weights, psf_rows, psf_cols, image, x)


def scatter_kernel(n, strips, g_ref, out_ref, got_core, got_pair, got_line, to_pair, to_line, rims,
                   got_rims, core_send, core_recv, pair_send, pair_recv, line_send, line_recv,
                   rim_send, rim_recv):
    f32, bf16 = jnp.float32, jnp.bfloat16
    line, split, join = places(n)
    me = lax.axis_index("exp")
    strip = lax.axis_index("strip")
    l, p, c = split(me)
    rows = out_ref.shape[0]
    above = {"strip": (strip + strips - 1) % strips}
    below = {"strip": (strip + 1) % strips}
    peers = [{"exp": join((l + q) % line, p, c)} for q in range(line)]
    pair = {"exp": join(l, 1 - p, c)}
    core = {"exp": join(l, p, 1 - c)}

    def push(src, dst, send, recv, device):
        copy = pltpu.make_async_remote_copy(
            src_ref=src, dst_ref=dst, send_sem=send, recv_sem=recv, device_id=device,
            device_id_type=MESH,
        )
        copy.start()
        return copy

    order = [0]
    for q in range(1, line // 2 + 1):
        order += [q, line - q] if q != line - q else [q]
    order = order[::-1]
    greet([above, below, pair, core] + peers[1:])
    swaps = {}
    for t, side in ((0, 1 - p), (1, p)):
        for q in order:
            at = t * line + q
            swaps[at] = push(g_ref.at[join((l + q) % line, side, 1 - c)], got_core.at[at],
                             core_send.at[at], core_recv.at[at], core)
    over = {}
    for q in order:
        swaps[q].wait_recv()
        to_pair[q] = (
            g_ref[join((l + q) % line, 1 - p, c)].astype(f32) + got_core[q].astype(f32)
        ).astype(bf16)
        over[q] = push(to_pair.at[q], got_pair.at[q], pair_send.at[q], pair_recv.at[q], pair)
    along = {}
    for q in order:
        swaps[line + q].wait_recv()
        over[q].wait_recv()
        part = (
            g_ref[join((l + q) % line, p, c)].astype(f32)
            + got_core[line + q].astype(f32)
            + got_pair[q].astype(f32)
        )
        if q:
            to_line[q] = part.astype(bf16)
            along[q] = push(to_line.at[q], got_line.at[q], line_send.at[q], line_recv.at[q],
                            peers[q])
        else:
            total = part
    for q in order[::-1][1:]:
        along[q].wait_recv()
        total = total + got_line[q].astype(f32)
    rims[0] = total[:RIM]
    rims[1] = total[rows + RIM :]
    out_ref[...] = total[RIM : rows + RIM]
    edges = [
        push(rims.at[0], got_rims.at[0], rim_send.at[0], rim_recv.at[0], above),
        push(rims.at[1], got_rims.at[1], rim_send.at[1], rim_recv.at[1], below),
    ]
    for copy in swaps.values():
        copy.wait_send()
    for copy in over.values():
        copy.wait_send()
    for copy in along.values():
        copy.wait_send()
    for copy in edges:
        copy.wait()
    has_below = jnp.where(strip < strips - 1, 1.0, 0.0)
    has_above = jnp.where(strip > 0, 1.0, 0.0)
    out_ref[rows - RIM :, :] = out_ref[rows - RIM :, :] + got_rims[0] * has_below
    out_ref[:RIM, :] = out_ref[:RIM, :] + got_rims[1] * has_above


def scatter(n, strips, g):
    line = n // 4
    high = g.shape[1]
    bf16 = jnp.bfloat16
    dma = pltpu.SemaphoreType.DMA
    return pl.pallas_call(
        functools.partial(scatter_kernel, n, strips),
        out_shape=jax.ShapeDtypeStruct((high - 2 * RIM, LANES), jnp.float32),
        in_specs=[VMEM],
        out_specs=VMEM,
        scratch_shapes=[
            pltpu.VMEM((2 * line, high, LANES), bf16),
            pltpu.VMEM((line, high, LANES), bf16),
            pltpu.VMEM((line, high, LANES), bf16),
            pltpu.VMEM((line, high, LANES), bf16),
            pltpu.VMEM((line, high, LANES), bf16),
            pltpu.VMEM((2, RIM, LANES), jnp.float32),
            pltpu.VMEM((2, RIM, LANES), jnp.float32),
            dma((2 * line,)), dma((2 * line,)), dma((line,)), dma((line,)), dma((line,)),
            dma((line,)), dma((2,)), dma((2,)),
        ],
        compiler_params=pltpu.CompilerParams(collective_id=1, has_side_effects=True),
    )(g)


def solution(mesh):
    n, strips = mesh.shape["exp"], mesh.shape["strip"]

    def local(model, images, footprint, psf_index, exposure_weight, psf_rows, psf_cols):
        x = gather(n, strips, model)
        g = compute(n, strips, footprint, psf_index, exposure_weight, psf_rows, psf_cols,
                    images[0], x)
        return model - step_size * scatter(n, strips, g)

    placed = (P("strip", "exp"), P("exp", "strip", None), P(), P(), P(), P(), P())
    return jax.shard_map(
        local, mesh=mesh, in_specs=placed, out_specs=P("strip", "exp"), check_vma=False
    )
```

time: 177 us -> 60.7 us (0.34)
  waiting for transfers between devices: 89.5 us -> 0 us
  Pallas kernels: 0 us -> 57.5 us
  matrix products: 30.6 us -> 0 us
  local copies, waits for them, and re-layouts: 20.2 us -> 1.36 us
  between operations: 13.8 us -> 0.03 us
  starting transfers between devices: 11.9 us -> 0 us
  other arithmetic: 10.2 us -> 1.57 us
    reduce_scatter x1 -> x0, waiting for transfers between devices: 60.6 us -> none  [local(): gradient = lax.psum_scatter(folded, 'exp', scatter_dimension=1, tiled=True)]
    pallas_call x0 -> x3, Pallas kernels: none -> 57.5 us  [the longest x1 22.2 us: gather(): pl.pallas_call(functools.partial(gather_kernel, n, strips), out_shape=jax...]
    dot_general x17 -> x0, matrix products: 30.6 us -> none  [the longest x7 10.4 us: banded(): jnp.einsum('...t,tio->...io', tap_values, onehot_table, precision=highest)]
    all_gather x1 -> x0, waiting for transfers between devices: 23.3 us -> none  [local(): whole_strip = lax.all_gather(model_half, 'exp', axis=1, tiled=True)]
    ppermute x4 -> x0, starting transfers between devices: 11.8 us -> none  [the longest x2 8.96 us: with_halo(): lax.ppermute(tail, axis, [(i, (i + 1) % count) for i in range(ends)])]
    convert_element_type x2 -> x0, local copies, waits for them, and re-layouts: 8.41 us -> none  [the longest x1 7.89 us: local(): adjoint = adjoint.astype(jnp.bfloat16).reshape(RANK * rows_here, width_all)]
    ppermute x4 -> x0, waiting for transfers between devices: 5.57 us -> none  [the longest x2 4.43 us: with_halo(): lax.ppermute(head, axis, [((i + 1) % count, i) for i in range(ends)])]
    dot_general x6 -> x0, local copies, waits for them, and re-layouts: 5.16 us -> none  [banded(): jnp.einsum('...t,tio->...io', tap_values, onehot_table, precision=highest)]
  transfers between devices with their start and end apart: 6 -> 0, of which waited for: 4 -> 0; matrix products, arithmetic and copies ran while one was open for 14% -> 0% of each run, Pallas kernels for 0% -> 0%
where the time goes in v1:
time: 60.7 us; the launch traced here: 60.4 us
  Pallas kernels  57.5 us (95%)
  other arithmetic  1.57 us (3%)
  local copies, waits for them, and re-layouts  1.36 us (2%)
    pallas_call x1, Pallas kernels, gather(): pl.pallas_call(functools.partial(gather_kernel, n, strips), out_shape=jax...  22.2 us
    pallas_call x1, Pallas kernels, scatter(): pl.pallas_call(functools.partial(scatter_kernel, n, strips), out_shape=ja...  19.4 us
    pallas_call x1, Pallas kernels, compute(): pl.pallas_call(functools.partial(compute_kernel, n, strips, rows), out_sh...  15.9 us
    sub x1, other arithmetic, local(): return model - step_size * scatter(n, strips, g)  1.57 us
    unnamed x3, local copies, waits for them, and re-layouts  1.36 us

profile of v1, /device:TPU:0, one launch (start us, length us, event | category | flops | bytes accessed | tf_op | source)
XLA Modules:
  0.0 60.4 jit_solution(8413419732925030872)
XLA Ops:
  0.0 1.4 %copy.8.footprint = s32[16,4]{1,0:T(8,128)} copy(s32[16,4]{0,1:T(4,128)} %param.9) | data formatting | bytes 512 | tf_op args[2]
  1.4 22.2 %shard_map.73.x_ref = bf16[16,288,128]{2,1,0:T(8,128)(2,1)} custom-call(f32[256,128]{1,0:T(8,128)} %model_ref.1), custom_call_target="tpu_custom_call" | custom-call | tf_op jit(solution)/shard_map/pallas_call | solution.py:106
  23.6 15.9 %shard_map.74.g_ref = bf16[16,288,128]{2,1,0:T(8,128)(2,1)} custom-call(s32[16,4]{1,0:T(8,128)} %copy.8.footprint, s32[16]{0:T(128)} %psf_index.1, f32[16]{0:T(128)} %weights.1, bf16[8,4,25]{2,1,0:T(4,128)(2,1)} %psf_rows.1, bf16[8,4,25]{2,1,0:T(4,128)(2,1)} %psf_cols.1, bf16[256,2048]{1,0:T(8,128)(2,1)} %bitcast.1, bf16[16,288,128]{2,1,0:T(8,128)(2,1)} %shard_map.73.x_ref), custom_call_target="tpu_custom_call" | custom-call | tf_op jit(solution)/shard_map/pallas_call | solution.py:236
  39.5 0.0 copy-start
  39.5 19.4 %shard_map.75 = f32[256,128]{1,0:T(8,128)} custom-call(bf16[16,288,128]{2,1,0:T(8,128)(2,1)} %shard_map.74.g_ref), custom_call_target="tpu_custom_call" | custom-call | tf_op jit(solution)/shard_map/pallas_call | solution.py:337
  58.9 0.0 copy-done
  58.9 1.6 %multiply_subtract_fusion = f32[256,128]{1,0:T(8,128)} fusion(f32[256,128]{1,0:T(8,128)S(1)} %copy-done, f32[256,128]{1,0:T(8,128)} %shard_map.75), kind=kLoop, calls=%fused_computation | loop fusion | flops 65536 | bytes 393216 | tf_op jit(solution)/shard_map/sub | solution.py:364
Async XLA Ops:
  39.5 19.4 %copy-start = (f32[256,128]{1,0:T(8,128)S(1)}, f32[256,128]{1,0:T(8,128)}, u32[]{:S(2)}) copy-start(f32[256,128]{1,0:T(8,128)} %model_ref.1) | copy-start | bytes 393220

commit v2 on v0

v2 whole, which is shorter than its diff:
```python
import functools

import jax
import jax.numpy as jnp
from jax import lax
from jax.experimental import pallas as pl
from jax.experimental.pallas import tpu as pltpu
from jax.sharding import PartitionSpec as P

RANK = 4
TAPS = 25
HALF = TAPS // 2
RIM = 16
LANES = 128
step_size = 0.25
MESH = pl.DeviceIdType.MESH
VMEM = pl.BlockSpec(memory_space=pltpu.VMEM)
SMEM = pl.BlockSpec(memory_space=pltpu.SMEM)


def places(n):
    line = n // 4
    if line < 8:
        split = lambda i: (i // 4, (i // 2) % 2, i % 2)
        join = lambda l, p, c: l * 4 + p * 2 + c
    else:
        split = lambda i: ((i // 2) % line, i // (2 * line), i % 2)
        join = lambda l, p, c: p * (2 * line) + l * 2 + c
    return line, split, join


def push(src, dst, send, recv, device):
    copy = pltpu.make_async_remote_copy(
        src_ref=src, dst_ref=dst, send_sem=send, recv_sem=recv, device_id=device,
        device_id_type=MESH,
    )
    copy.start()
    return copy


def greet(devices):
    barrier = pltpu.get_barrier_semaphore()
    for device in devices:
        pl.semaphore_signal(barrier, inc=1, device_id=device, device_id_type=MESH)
    pl.semaphore_wait(barrier, len(devices))


def step_kernel(n, strips, model_ref, footprint, psf_index, weights, psf_rows, psf_cols, image_ref,
                out_ref, image, x, edge, lift, drop, fore, back, pred, res, g, rim, got_rim,
                got_core, to_pair, got_pair, to_line, got_line, image_sem, line_sems, pair_sems,
                core_sems, edge_sems, swap_sems, over_sems, along_sems, rim_sems):
    f32, bf16 = jnp.float32, jnp.bfloat16
    line, split, join = places(n)
    me = lax.axis_index("exp")
    strip = lax.axis_index("strip")
    l, p, c = split(me)
    rows = model_ref.shape[0]
    wide = n * LANES
    parts = rows // LANES
    window = LANES + 2 * RIM
    above, below = (strip + strips - 1) % strips, (strip + 1) % strips
    peers = [{"exp": join((l + q) % line, p, c)} for q in range(line)]
    partner = join(l, p, 1 - c)
    pair = {"exp": join(l, 1 - p, c)}
    core = {"exp": partner}
    aboves = [{"strip": above, "exp": me}, {"strip": above, "exp": partner}]
    belows = [{"strip": below, "exp": me}, {"strip": below, "exp": partner}]

    order = [0]
    for q in range(1, line // 2 + 1):
        order += [q, line - q] if q != line - q else [q]

    fetch = pltpu.make_async_copy(image_ref, image, image_sem)
    fetch.start()
    x[me] = model_ref[...].astype(bf16)
    greet(aboves + belows + [pair, core] + peers[1:])
    along, over, across, edges = {}, {}, {}, {}

    def spread_slot(at, slot):
        across[at] = push(x.at[slot], x.at[slot], core_sems.at[0, at], core_sems.at[1, at], core)
        for cc in range(2):
            edges[at, cc, 0] = push(
                x.at[slot, pl.ds(rows - RIM, RIM)], edge.at[slot, 0],
                edge_sems.at[0, at, cc, 0], edge_sems.at[1, at, cc, 0], belows[cc],
            )
            edges[at, cc, 1] = push(
                x.at[slot, pl.ds(0, RIM)], edge.at[slot, 1],
                edge_sems.at[0, at, cc, 1], edge_sems.at[1, at, cc, 1], aboves[cc],
            )

    def forward_line(q):
        slot = join((l + line - q) % line, p, c)
        if q:
            along[q].wait_recv()
        over[q] = push(x.at[slot], x.at[slot], pair_sems.at[0, q], pair_sems.at[1, q], pair)
        spread_slot(q, slot)

    def forward_pair(q):
        over[q].wait_recv()
        spread_slot(line + q, join((l + line - q) % line, 1 - p, c))

    for q in order[:0:-1]:
        along[q] = push(x.at[me], x.at[me], line_sems.at[0, q], line_sems.at[1, q], peers[q])
    forward_line(0)

    chosen = psf_index[me]

    def taps_of(table):
        total = jnp.zeros((RANK, TAPS), f32)
        for b in range(table.shape[0]):
            total = total + jnp.where(chosen == b, table[b].astype(f32), 0.0)
        return total.astype(bf16)

    tap = lax.broadcasted_iota(jnp.int32, (TAPS, 384), 0)
    lane = lax.broadcasted_iota(jnp.int32, (TAPS, 384), 1)
    same = (tap == lane).astype(f32).astype(bf16)
    mirror = (tap + lane == TAPS - 1).astype(f32).astype(bf16)
    row_taps = jnp.dot(taps_of(psf_rows), same, preferred_element_type=f32)
    col_taps = taps_of(psf_cols)
    col_fore = jnp.dot(col_taps, mirror, preferred_element_type=f32)
    col_back = jnp.dot(col_taps, same, preferred_element_type=f32)

    def slanted(vector, width, shift):
        spread = jnp.broadcast_to(vector[:, :width], (LANES, width))
        return pltpu.roll(pltpu.roll(spread, 0, 1, stride=1, stride_axis=0), shift, 1)

    none = jnp.zeros((LANES, LANES), bf16)
    for k in range(RANK):
        band = slanted(row_taps[k : k + 1], 256, RIM - HALF)
        lift[k * LANES : (k + 1) * LANES, :] = band[:, :window].astype(bf16)
        drop[:, k * LANES : (k + 1) * LANES] = band.T[:window].astype(bf16)
        band = slanted(col_fore[k : k + 1], 384, LANES - HALF).astype(bf16)
        fore[2 * k * LANES : (2 * k + 1) * LANES, :] = jnp.concatenate([band, none], axis=1)
        fore[(2 * k + 1) * LANES : (2 * k + 2) * LANES, :] = jnp.concatenate([none, band], axis=1)
        band = slanted(col_back[k : k + 1], 384, LANES - HALF).astype(bf16)
        for w in range(4):
            for o in range(2):
                d = w - o
                piece = band[:, (2 - d) * LANES : (3 - d) * LANES] if 0 <= d <= 2 else none
                at = (2 * k + o) * LANES
                back[w * LANES : (w + 1) * LANES, at : at + LANES] = piece
    pred[...] = jnp.zeros_like(pred)
    res[:, :LANES] = jnp.zeros((rows, LANES), bf16)
    res[:, wide + LANES :] = jnp.zeros((rows, LANES), bf16)

    top = jnp.where(strip > 0, 1.0, 0.0)
    bottom = jnp.where(strip < strips - 1, 1.0, 0.0)

    def fore_step(group):
        def step(side, carry):
            left = join(group, side, 0)
            right = left + 1
            upper = jnp.concatenate([edge[left, 0], edge[right, 0]], axis=1)
            lower = jnp.concatenate([edge[left, 1], edge[right, 1]], axis=1)
            upper = (upper.astype(f32) * top).astype(bf16)
            lower = (lower.astype(f32) * bottom).astype(bf16)
            middle = jnp.concatenate([x[left], x[right]], axis=1)
            cells = jnp.concatenate([upper, middle, lower], axis=0)
            passes = []
            for s in range(parts):
                out = jnp.dot(lift[...], cells[s * LANES : s * LANES + window],
                              preferred_element_type=f32).astype(bf16)
                passes.append(jnp.concatenate(
                    [out[k * LANES : (k + 1) * LANES] for k in range(RANK)], axis=1))
            stack = jnp.concatenate(passes, axis=0)
            at = pl.ds(pl.multiple_of(left * LANES, 2 * LANES), 4 * LANES)
            pred[:, at] = pred[:, at] + jnp.dot(stack, fore[...], preferred_element_type=f32)
            return carry

        lax.fori_loop(0, 2, step, 0)

    lines_done, pairs_done = 1, 0
    for i, q in enumerate(order):
        while lines_done < min(line, i + 3):
            forward_line(order[lines_done])
            lines_done += 1
        while pairs_done < min(line, i + 2 if i else 1):
            forward_pair(order[pairs_done])
            pairs_done += 1
        for at in (q, line + q):
            across[at].wait_recv()
            for cc in range(2):
                for side in range(2):
                    edges[at, cc, side].wait_recv()
        fore_step((l + line - q) % line)

    fetch.wait()
    weight = weights[me]
    first_row, last_row = footprint[0, me], footprint[1, me]
    first_col, last_col = footprint[2, me], footprint[3, me]
    row_at = lax.broadcasted_iota(jnp.int32, (rows, 256), 0) + strip * rows
    col_at = lax.broadcasted_iota(jnp.int32, (rows, 256), 1)
    row_ok = (row_at >= first_row) & (row_at < last_row)

    def residual_step(b, carry):
        begin = pl.multiple_of(256 * b, 256)
        inner = pl.ds(pl.multiple_of(256 * b + LANES, LANES), 256)
        inside = row_ok & (col_at >= first_col - begin) & (col_at < last_col - begin)
        value = weight * (pred[:, inner] - image[:, pl.ds(begin, 256)].astype(f32))
        res[:, inner] = jnp.where(inside, value, 0.0).astype(bf16)
        return carry

    lax.fori_loop(0, n // 2, residual_step, 0)

    def back_step(group):
        def step(side, carry):
            left = join(group, side, 0)
            cells = res[:, pl.ds(pl.multiple_of(left * LANES, 2 * LANES), 4 * LANES)]
            spread = jnp.dot(cells, back[...], preferred_element_type=f32).astype(bf16)
            pieces = []
            for s in range(parts):
                part = spread[s * LANES : (s + 1) * LANES]
                stack = jnp.concatenate(
                    [part[:, k * 256 : (k + 1) * 256] for k in range(RANK)], axis=0)
                pieces.append(jnp.dot(drop[...], stack, preferred_element_type=f32))
            joined = [pieces[0][RIM:LANES]]
            for s in range(1, parts):
                joined.append(pieces[s - 1][LANES:] + pieces[s][: 2 * RIM])
                joined.append(pieces[s][2 * RIM : LANES])
            joined.append(pieces[-1][LANES : LANES + RIM])
            total = jnp.concatenate(joined, axis=0).astype(bf16)
            first, last = pieces[0][:RIM].astype(bf16), pieces[-1][LANES + RIM :].astype(bf16)
            for o in range(2):
                cols = slice(o * LANES, (o + 1) * LANES)
                g[left + o] = total[:, cols]
                rim[left + o, 0] = first[:, cols]
                rim[left + o, 1] = last[:, cols]
            return carry

        lax.fori_loop(0, 2, step, 0)

    swaps, rims, onward, home = {}, {}, {}, {}

    def send_group(q):
        group = (l + q) % line
        back_step(group)
        for t, side in ((0, 1 - p), (1, p)):
            at = t * line + q
            swaps[at] = push(g.at[join(group, side, 1 - c)], got_core.at[at],
                             swap_sems.at[0, at], swap_sems.at[1, at], core)
            for cc, whose in ((0, c), (1, 1 - c)):
                slot = join(group, side, whose)
                rims[at, cc, 0] = push(
                    rim.at[slot, 0], got_rim.at[at, cc, 0],
                    rim_sems.at[0, at, cc, 0], rim_sems.at[1, at, cc, 0], aboves[cc])
                rims[at, cc, 1] = push(
                    rim.at[slot, 1], got_rim.at[at, cc, 1],
                    rim_sems.at[0, at, cc, 1], rim_sems.at[1, at, cc, 1], belows[cc])

    def chip_sum(at, slot):
        swaps[at].wait_recv()
        for cc in range(2):
            for side in range(2):
                rims[at, cc, side].wait_recv()
        total = g[slot].astype(f32) + got_core[at].astype(f32)
        low = (got_rim[at, 0, 0].astype(f32) + got_rim[at, 1, 0].astype(f32)) * bottom
        high = (got_rim[at, 0, 1].astype(f32) + got_rim[at, 1, 1].astype(f32)) * top
        return jnp.concatenate(
            [total[:RIM] + high, total[RIM : rows - RIM], total[rows - RIM :] + low], axis=0)

    def send_pair(q):
        to_pair[q] = chip_sum(q, join((l + q) % line, 1 - p, c)).astype(bf16)
        onward[q] = push(to_pair.at[q], got_pair.at[q], over_sems.at[0, q], over_sems.at[1, q],
                         pair)

    def send_line(q):
        total = chip_sum(line + q, join((l + q) % line, p, c))
        onward[q].wait_recv()
        total = total + got_pair[q].astype(f32)
        if q:
            to_line[q] = total.astype(bf16)
            home[q] = push(to_line.at[q], got_line.at[q], along_sems.at[0, q],
                           along_sems.at[1, q], peers[q])
        return total

    total = None
    for i in range(line + 2):
        if i < line:
            send_group(order[line - 1 - i])
        if 1 <= i < line + 1:
            send_pair(order[line - i])
        if i >= 2:
            total = send_line(order[line + 1 - i])
    for q in order[:0:-1]:
        home[q].wait_recv()
        total = total + got_line[q].astype(f32)
    out_ref[...] = total
    for group in (along, over, across, edges, swaps, rims, onward, home):
        for copy in group.values():
            copy.wait_send()


def solution(mesh):
    n, strips = mesh.shape["exp"], mesh.shape["strip"]
    line = n // 4
    f32, bf16 = jnp.float32, jnp.bfloat16
    dma = pltpu.SemaphoreType.DMA
    window = LANES + 2 * RIM

    def local(model, images, footprint, psf_index, exposure_weight, psf_rows, psf_cols):
        rows = model.shape[0]
        blocks = lambda count: pltpu.VMEM((count, rows, LANES), bf16)
        gradient = pl.pallas_call(
            functools.partial(step_kernel, n, strips),
            out_shape=jax.ShapeDtypeStruct(model.shape, f32),
            in_specs=[VMEM, SMEM, SMEM, SMEM, VMEM, VMEM, pl.BlockSpec(memory_space=pl.ANY)],
            out_specs=VMEM,
            scratch_shapes=[
                pltpu.VMEM((rows, n * LANES), bf16),
                blocks(n),
                pltpu.VMEM((n, 2, RIM, LANES), bf16),
                pltpu.VMEM((RANK * LANES, window), bf16),
                pltpu.VMEM((window, RANK * LANES), bf16),
                pltpu.VMEM((RANK * 2 * LANES, 4 * LANES), bf16),
                pltpu.VMEM((4 * LANES, RANK * 2 * LANES), bf16),
                pltpu.VMEM((rows, (n + 2) * LANES), f32),
                pltpu.VMEM((rows, (n + 2) * LANES), bf16),
                blocks(n),
                pltpu.VMEM((n, 2, RIM, LANES), bf16),
                pltpu.VMEM((2 * line, 2, 2, RIM, LANES), bf16),
                blocks(2 * line), blocks(line), blocks(line), blocks(line), blocks(line),
                dma, dma((2, line)), dma((2, line)), dma((2, 2 * line)),
                dma((2, 2 * line, 2, 2)), dma((2, 2 * line)), dma((2, line)), dma((2, line)),
                dma((2, 2 * line, 2, 2)),
            ],
            compiler_params=pltpu.CompilerParams(collective_id=0, has_side_effects=True),
        )(model, footprint.T, psf_index, exposure_weight, psf_rows, psf_cols, images[0])
        return model - step_size * gradient

    placed = (P("strip", "exp"), P("exp", "strip", None), P(), P(), P(), P(), P())
    return jax.shard_map(
        local, mesh=mesh, in_specs=placed, out_specs=P("strip", "exp"), check_vma=False
    )
```

time: 177 us -> 45.6 us (0.26)
  waiting for transfers between devices: 89.5 us -> 0 us
  Pallas kernels: 0 us -> 43.8 us
  matrix products: 30.6 us -> 0 us
  local copies, waits for them, and re-layouts: 20.2 us -> 0.01 us
  between operations: 13.8 us -> 0.02 us
  starting transfers between devices: 11.9 us -> 0 us
  other arithmetic: 10.2 us -> 1.57 us
    reduce_scatter x1 -> x0, waiting for transfers between devices: 60.6 us -> none  [local(): gradient = lax.psum_scatter(folded, 'exp', scatter_dimension=1, tiled=True)]
    pallas_call x0 -> x1, Pallas kernels: none -> 43.8 us  [local(): pl.pallas_call(functools.partial(step_kernel, n, strips), out_shape=jax.S...]
    dot_general x17 -> x0, matrix products: 30.6 us -> none  [the longest x7 10.4 us: banded(): jnp.einsum('...t,tio->...io', tap_values, onehot_table, precision=highest)]
    all_gather x1 -> x0, waiting for transfers between devices: 23.3 us -> none  [local(): whole_strip = lax.all_gather(model_half, 'exp', axis=1, tiled=True)]
    ppermute x4 -> x0, starting transfers between devices: 11.8 us -> none  [the longest x2 8.96 us: with_halo(): lax.ppermute(tail, axis, [(i, (i + 1) % count) for i in range(ends)])]
    convert_element_type x2 -> x0, local copies, waits for them, and re-layouts: 8.41 us -> none  [the longest x1 7.89 us: local(): adjoint = adjoint.astype(jnp.bfloat16).reshape(RANK * rows_here, width_all)]
    ppermute x4 -> x0, waiting for transfers between devices: 5.57 us -> none  [the longest x2 4.43 us: with_halo(): lax.ppermute(head, axis, [((i + 1) % count, i) for i in range(ends)])]
    dot_general x6 -> x0, local copies, waits for them, and re-layouts: 5.16 us -> none  [banded(): jnp.einsum('...t,tio->...io', tap_values, onehot_table, precision=highest)]
  transfers between devices with their start and end apart: 6 -> 0, of which waited for: 4 -> 0; matrix products, arithmetic and copies ran while one was open for 14% -> 0% of each run, Pallas kernels for 0% -> 0%
where the time goes in v2:
time: 45.6 us; the launch traced here: 45.4 us
  Pallas kernels  43.8 us (96%)
  other arithmetic  1.57 us (3%)
    pallas_call x1, Pallas kernels, local(): pl.pallas_call(functools.partial(step_kernel, n, strips), out_shape=jax.S...  43.8 us
    sub x1, other arithmetic, local(): return model - step_size * gradient  1.57 us

profile of v2, /device:TPU:0, one launch (start us, length us, event | category | flops | bytes accessed | tf_op | source)
XLA Modules:
  0.0 45.4 jit_solution(3076131340394108959)
XLA Ops:
  0.0 0.0 copy-start
  0.0 43.8 %shard_map.73 = f32[256,128]{1,0:T(8,128)} custom-call(f32[256,128]{1,0:T(8,128)} %model_ref.1, s32[4,16]{1,0:T(4,128)} %bitcast.3, s32[16]{0:T(128)} %psf_index.1, f32[16]{0:T(128)} %weights.1, bf16[8,4,25]{2,1,0:T(4,128)(2,1)} %psf_rows.1, bf16[8,4,25]{2,1,0:T(4,128)(2,1)} %psf_cols.1, bf16[256,2048]{1,0:T(8,128)(2,1)} %bitcast.2), custom_call_target="tpu_custom_call" | custom-call | tf_op jit(solution)/shard_map/pallas_call | solution.py:303
  43.8 0.0 copy-done
  43.8 1.6 %multiply_subtract_fusion = f32[256,128]{1,0:T(8,128)} fusion(f32[256,128]{1,0:T(8,128)S(1)} %copy-done, f32[256,128]{1,0:T(8,128)} %shard_map.73), kind=kLoop, calls=%fused_computation | loop fusion | flops 65536 | bytes 393216 | tf_op jit(solution)/shard_map/sub | solution.py:328
Async XLA Ops:
  0.0 43.8 %copy-start = (f32[256,128]{1,0:T(8,128)S(1)}, f32[256,128]{1,0:T(8,128)}, u32[]{:S(2)}) copy-start(f32[256,128]{1,0:T(8,128)} %model_ref.1) | copy-start | bytes 393220

commit v3 on v2

--- a/solution.py
+++ b/solution.py
@@ -48,7 +48,8 @@
 def step_kernel(n, strips, model_ref, footprint, psf_index, weights, psf_rows, psf_cols, image_ref,
                 out_ref, image, x, edge, lift, drop, fore, back, pred, res, g, rim, got_rim,
                 got_core, to_pair, got_pair, to_line, got_line, image_sem, line_sems, pair_sems,
-                core_sems, edge_sems, swap_sems, over_sems, along_sems, rim_sems):
+                core_sems, halo_sems, rim_line_sems, rim_pair_sems,
+                rim_core_sems, swap_sems, over_sems, along_sems, rim_sems):
     f32, bf16 = jnp.float32, jnp.bfloat16
     line, split, join = places(n)
     me = lax.axis_index("exp")
@@ -76,32 +77,46 @@
     greet(aboves + belows + [pair, core] + peers[1:])
     along, over, across, edges = {}, {}, {}, {}
 
-    def spread_slot(at, slot):
+    def send_core(at, slot):
         across[at] = push(x.at[slot], x.at[slot], core_sems.at[0, at], core_sems.at[1, at], core)
-        for cc in range(2):
-            edges[at, cc, 0] = push(
-                x.at[slot, pl.ds(rows - RIM, RIM)], edge.at[slot, 0],
-                edge_sems.at[0, at, cc, 0], edge_sems.at[1, at, cc, 0], belows[cc],
-            )
-            edges[at, cc, 1] = push(
-                x.at[slot, pl.ds(0, RIM)], edge.at[slot, 1],
-                edge_sems.at[0, at, cc, 1], edge_sems.at[1, at, cc, 1], aboves[cc],
-            )
+
+    def send_core_edge(at, slot):
+        edges["core", at] = push(edge.at[slot], edge.at[slot], rim_core_sems.at[0, at],
+                                 rim_core_sems.at[1, at], core)
+
+    def send_over(q, slot):
+        over[q] = push(x.at[slot], x.at[slot], pair_sems.at[0, q], pair_sems.at[1, q], pair)
+
+    def send_over_edge(q, slot):
+        edges["pair", q] = push(edge.at[slot], edge.at[slot], rim_pair_sems.at[0, q],
+                                rim_pair_sems.at[1, q], pair)
 
     def forward_line(q):
         slot = join((l + line - q) % line, p, c)
-        if q:
-            along[q].wait_recv()
-        over[q] = push(x.at[slot], x.at[slot], pair_sems.at[0, q], pair_sems.at[1, q], pair)
-        spread_slot(q, slot)
+        along[q].wait_recv()
+        send_over(q, slot)
+        send_core(q, slot)
+        edges["line", q].wait_recv()
+        send_over_edge(q, slot)
+        send_core_edge(q, slot)
 
     def forward_pair(q):
+        slot = join((l + line - q) % line, 1 - p, c)
         over[q].wait_recv()
-        spread_slot(line + q, join((l + line - q) % line, 1 - p, c))
-
-    for q in order[:0:-1]:
+        send_core(line + q, slot)
+        edges["pair", q].wait_recv()
+        send_core_edge(line + q, slot)
+
+    halos = [
+        push(x.at[me, pl.ds(rows - RIM, RIM)], edge.at[me, 0], halo_sems.at[0, 0],
+             halo_sems.at[1, 0], {"strip": below}),
+        push(x.at[me, pl.ds(0, RIM)], edge.at[me, 1], halo_sems.at[0, 1], halo_sems.at[1, 1],
+             {"strip": above}),
+    ]
+    for q in order[1:]:
         along[q] = push(x.at[me], x.at[me], line_sems.at[0, q], line_sems.at[1, q], peers[q])
-    forward_line(0)
+    send_over(0, me)
+    send_core(0, me)
 
     chosen = psf_index[me]
 
@@ -128,10 +143,21 @@
     for k in range(RANK):
         band = slanted(row_taps[k : k + 1], 256, RIM - HALF)
         lift[k * LANES : (k + 1) * LANES, :] = band[:, :window].astype(bf16)
-        drop[:, k * LANES : (k + 1) * LANES] = band.T[:window].astype(bf16)
         band = slanted(col_fore[k : k + 1], 384, LANES - HALF).astype(bf16)
         fore[2 * k * LANES : (2 * k + 1) * LANES, :] = jnp.concatenate([band, none], axis=1)
         fore[(2 * k + 1) * LANES : (2 * k + 2) * LANES, :] = jnp.concatenate([none, band], axis=1)
+
+    for copy in halos:
+        copy.wait()
+    for q in order[1:]:
+        edges["line", q] = push(edge.at[me], edge.at[me], rim_line_sems.at[0, q],
+                                rim_line_sems.at[1, q], peers[q])
+    send_over_edge(0, me)
+    send_core_edge(0, me)
+
+    for k in range(RANK):
+        band = slanted(row_taps[k : k + 1], 256, RIM - HALF)
+        drop[:, k * LANES : (k + 1) * LANES] = band.T[:window].astype(bf16)
         band = slanted(col_back[k : k + 1], 384, LANES - HALF).astype(bf16)
         for w in range(4):
             for o in range(2):
@@ -146,43 +172,46 @@
     top = jnp.where(strip > 0, 1.0, 0.0)
     bottom = jnp.where(strip < strips - 1, 1.0, 0.0)
 
-    def fore_step(group):
-        def step(side, carry):
-            left = join(group, side, 0)
-            right = left + 1
-            upper = jnp.concatenate([edge[left, 0], edge[right, 0]], axis=1)
-            lower = jnp.concatenate([edge[left, 1], edge[right, 1]], axis=1)
-            upper = (upper.astype(f32) * top).astype(bf16)
-            lower = (lower.astype(f32) * bottom).astype(bf16)
-            middle = jnp.concatenate([x[left], x[right]], axis=1)
-            cells = jnp.concatenate([upper, middle, lower], axis=0)
-            passes = []
-            for s in range(parts):
-                out = jnp.dot(lift[...], cells[s * LANES : s * LANES + window],
-                              preferred_element_type=f32).astype(bf16)
-                passes.append(jnp.concatenate(
-                    [out[k * LANES : (k + 1) * LANES] for k in range(RANK)], axis=1))
-            stack = jnp.concatenate(passes, axis=0)
-            at = pl.ds(pl.multiple_of(left * LANES, 2 * LANES), 4 * LANES)
-            pred[:, at] = pred[:, at] + jnp.dot(stack, fore[...], preferred_element_type=f32)
-            return carry
-
-        lax.fori_loop(0, 2, step, 0)
-
-    lines_done, pairs_done = 1, 0
-    for i, q in enumerate(order):
-        while lines_done < min(line, i + 3):
-            forward_line(order[lines_done])
-            lines_done += 1
-        while pairs_done < min(line, i + 2 if i else 1):
-            forward_pair(order[pairs_done])
-            pairs_done += 1
-        for at in (q, line + q):
-            across[at].wait_recv()
-            for cc in range(2):
-                for side in range(2):
-                    edges[at, cc, side].wait_recv()
-        fore_step((l + line - q) % line)
+    def fore_step(at, group, side):
+        across[at].wait_recv()
+        edges["core", at].wait_recv()
+        left = join(group, side, 0)
+        right = left + 1
+        upper = jnp.concatenate([edge[left, 0], edge[right, 0]], axis=1)
+        lower = jnp.concatenate([edge[left, 1], edge[right, 1]], axis=1)
+        upper = (upper.astype(f32) * top).astype(bf16)
+        lower = (lower.astype(f32) * bottom).astype(bf16)
+        middle = jnp.concatenate([x[left], x[right]], axis=1)
+        cells = jnp.concatenate([upper, middle, lower], axis=0)
+        passes = []
+        for s in range(parts):
+            out = jnp.dot(lift[...], cells[s * LANES : s * LANES + window],
+                          preferred_element_type=f32).astype(bf16)
+            passes.append(jnp.concatenate(
+                [out[k * LANES : (k + 1) * LANES] for k in range(RANK)], axis=1))
+        stack = jnp.concatenate(passes, axis=0)
+        at = pl.ds(pl.multiple_of(left * LANES, 2 * LANES), 4 * LANES)
+        pred[:, at] = pred[:, at] + jnp.dot(stack, fore[...], preferred_element_type=f32)
+
+    def near_step(q):
+        fore_step(q, (l + line - q) % line, p)
+
+    def far_step(q):
+        fore_step(line + q, (l + line - q) % line, 1 - p)
+
+    near_step(0)
+    forward_pair(0)
+    for q in order[1:3]:
+        forward_line(q)
+    far_step(0)
+    for i in range(1, line):
+        near_step(order[i])
+        forward_pair(order[i])
+        if i + 2 < line:
+            forward_line(order[i + 2])
+        if i >= 2:
+            far_step(order[i - 1])
+    far_step(order[-1])
 
     fetch.wait()
     weight = weights[me]
@@ -202,40 +231,36 @@
 
     lax.fori_loop(0, n // 2, residual_step, 0)
 
-    def back_step(group):
-        def step(side, carry):
-            left = join(group, side, 0)
-            cells = res[:, pl.ds(pl.multiple_of(left * LANES, 2 * LANES), 4 * LANES)]
-            spread = jnp.dot(cells, back[...], preferred_element_type=f32).astype(bf16)
-            pieces = []
-            for s in range(parts):
-                part = spread[s * LANES : (s + 1) * LANES]
-                stack = jnp.concatenate(
-                    [part[:, k * 256 : (k + 1) * 256] for k in range(RANK)], axis=0)
-                pieces.append(jnp.dot(drop[...], stack, preferred_element_type=f32))
-            joined = [pieces[0][RIM:LANES]]
-            for s in range(1, parts):
-                joined.append(pieces[s - 1][LANES:] + pieces[s][: 2 * RIM])
-                joined.append(pieces[s][2 * RIM : LANES])
-            joined.append(pieces[-1][LANES : LANES + RIM])
-            total = jnp.concatenate(joined, axis=0).astype(bf16)
-            first, last = pieces[0][:RIM].astype(bf16), pieces[-1][LANES + RIM :].astype(bf16)
-            for o in range(2):
-                cols = slice(o * LANES, (o + 1) * LANES)
-                g[left + o] = total[:, cols]
-                rim[left + o, 0] = first[:, cols]
-                rim[left + o, 1] = last[:, cols]
-            return carry
-
-        lax.fori_loop(0, 2, step, 0)
+    def back_step(group, side):
+        left = join(group, side, 0)
+        cells = res[:, pl.ds(pl.multiple_of(left * LANES, 2 * LANES), 4 * LANES)]
+        spread = jnp.dot(cells, back[...], preferred_element_type=f32).astype(bf16)
+        pieces = []
+        for s in range(parts):
+            part = spread[s * LANES : (s + 1) * LANES]
+            stack = jnp.concatenate(
+                [part[:, k * 256 : (k + 1) * 256] for k in range(RANK)], axis=0)
+            pieces.append(jnp.dot(drop[...], stack, preferred_element_type=f32))
+        joined = [pieces[0][RIM:LANES]]
+        for s in range(1, parts):
+            joined.append(pieces[s - 1][LANES:] + pieces[s][: 2 * RIM])
+            joined.append(pieces[s][2 * RIM : LANES])
+        joined.append(pieces[-1][LANES : LANES + RIM])
+        total = jnp.concatenate(joined, axis=0).astype(bf16)
+        first, last = pieces[0][:RIM].astype(bf16), pieces[-1][LANES + RIM :].astype(bf16)
+        for o in range(2):
+            cols = slice(o * LANES, (o + 1) * LANES)
+            g[left + o] = total[:, cols]
+            rim[left + o, 0] = first[:, cols]
+            rim[left + o, 1] = last[:, cols]
 
     swaps, rims, onward, home = {}, {}, {}, {}
 
     def send_group(q):
         group = (l + q) % line
-        back_step(group)
         for t, side in ((0, 1 - p), (1, p)):
             at = t * line + q
+            back_step(group, side)
             swaps[at] = push(g.at[join(group, side, 1 - c)], got_core.at[at],
                              swap_sems.at[0, at], swap_sems.at[1, at], core)
             for cc, whose in ((0, c), (1, 1 - c)):
@@ -320,7 +345,8 @@
                 pltpu.VMEM((2 * line, 2, 2, RIM, LANES), bf16),
                 blocks(2 * line), blocks(line), blocks(line), blocks(line), blocks(line),
                 dma, dma((2, line)), dma((2, line)), dma((2, 2 * line)),
-                dma((2, 2 * line, 2, 2)), dma((2, 2 * line)), dma((2, line)), dma((2, line)),
+                dma((2, 2)), dma((2, line)), dma((2, line)), dma((2, 2 * line)),
+                dma((2, 2 * line)), dma((2, line)), dma((2, line)),
                 dma((2, 2 * line, 2, 2)),
             ],
             compiler_params=pltpu.CompilerParams(collective_id=0, has_side_effects=True),

time: 45.6 us -> 40 us (0.88)
  Pallas kernels: 43.8 us -> 38.2 us
    pallas_call x1, Pallas kernels: 43.8 us -> 38.2 us  [local(): pl.pallas_call(functools.partial(step_kernel, n, strips), out_shape=jax.S...]
where the time goes in v3:
time: 40 us; the launch traced here: 39.8 us
  Pallas kernels  38.2 us (96%)
  other arithmetic  1.57 us (4%)
    pallas_call x1, Pallas kernels, local(): pl.pallas_call(functools.partial(step_kernel, n, strips), out_shape=jax.S...  38.2 us
    sub x1, other arithmetic, local(): return model - step_size * gradient  1.57 us

profile of v3, /device:TPU:0, one launch (start us, length us, event | category | flops | bytes accessed | tf_op | source)
XLA Modules:
  0.0 39.8 jit_solution(12646270463539101313)
XLA Ops:
  0.0 0.0 copy-start
  0.0 38.2 %shard_map.73 = f32[256,128]{1,0:T(8,128)} custom-call(f32[256,128]{1,0:T(8,128)} %model_ref.1, s32[4,16]{1,0:T(4,128)} %bitcast.3, s32[16]{0:T(128)} %psf_index.1, f32[16]{0:T(128)} %weights.1, bf16[8,4,25]{2,1,0:T(4,128)(2,1)} %psf_rows.1, bf16[8,4,25]{2,1,0:T(4,128)(2,1)} %psf_cols.1, bf16[256,2048]{1,0:T(8,128)(2,1)} %bitcast.2), custom_call_target="tpu_custom_call" | custom-call | tf_op jit(solution)/shard_map/pallas_call | solution.py:328
  38.2 0.0 copy-done
  38.3 1.6 %multiply_subtract_fusion = f32[256,128]{1,0:T(8,128)} fusion(f32[256,128]{1,0:T(8,128)S(1)} %copy-done, f32[256,128]{1,0:T(8,128)} %shard_map.73), kind=kLoop, calls=%fused_computation | loop fusion | flops 65536 | bytes 393216 | tf_op jit(solution)/shard_map/sub | solution.py:354
Async XLA Ops:
  0.0 38.2 %copy-start = (f32[256,128]{1,0:T(8,128)S(1)}, f32[256,128]{1,0:T(8,128)}, u32[]{:S(2)}) copy-start(f32[256,128]{1,0:T(8,128)} %model_ref.1) | copy-start | bytes 393220

commit v4 on v3

--- a/solution.py
+++ b/solution.py
@@ -256,21 +256,21 @@
 
     swaps, rims, onward, home = {}, {}, {}, {}
 
-    def send_group(q):
+    def send_side(q, t):
         group = (l + q) % line
-        for t, side in ((0, 1 - p), (1, p)):
-            at = t * line + q
-            back_step(group, side)
-            swaps[at] = push(g.at[join(group, side, 1 - c)], got_core.at[at],
-                             swap_sems.at[0, at], swap_sems.at[1, at], core)
-            for cc, whose in ((0, c), (1, 1 - c)):
-                slot = join(group, side, whose)
-                rims[at, cc, 0] = push(
-                    rim.at[slot, 0], got_rim.at[at, cc, 0],
-                    rim_sems.at[0, at, cc, 0], rim_sems.at[1, at, cc, 0], aboves[cc])
-                rims[at, cc, 1] = push(
-                    rim.at[slot, 1], got_rim.at[at, cc, 1],
-                    rim_sems.at[0, at, cc, 1], rim_sems.at[1, at, cc, 1], belows[cc])
+        side = (1 - p, p)[t]
+        at = t * line + q
+        back_step(group, side)
+        swaps[at] = push(g.at[join(group, side, 1 - c)], got_core.at[at],
+                         swap_sems.at[0, at], swap_sems.at[1, at], core)
+        for cc, whose in ((0, c), (1, 1 - c)):
+            slot = join(group, side, whose)
+            rims[at, cc, 0] = push(
+                rim.at[slot, 0], got_rim.at[at, cc, 0],
+                rim_sems.at[0, at, cc, 0], rim_sems.at[1, at, cc, 0], aboves[cc])
+            rims[at, cc, 1] = push(
+                rim.at[slot, 1], got_rim.at[at, cc, 1],
+                rim_sems.at[0, at, cc, 1], rim_sems.at[1, at, cc, 1], belows[cc])
 
     def chip_sum(at, slot):
         swaps[at].wait_recv()
@@ -298,14 +298,17 @@
                            along_sems.at[1, q], peers[q])
         return total
 
-    total = None
-    for i in range(line + 2):
-        if i < line:
-            send_group(order[line - 1 - i])
-        if 1 <= i < line + 1:
-            send_pair(order[line - i])
-        if i >= 2:
-            total = send_line(order[line + 1 - i])
+    away = order[::-1]
+    for i, q in enumerate(away):
+        send_side(q, 0)
+        if i:
+            send_pair(away[i - 1])
+    send_side(away[0], 1)
+    send_pair(away[-1])
+    for i in range(1, line):
+        send_side(away[i], 1)
+        send_line(away[i - 1])
+    total = send_line(away[-1])
     for q in order[:0:-1]:
         home[q].wait_recv()
         total = total + got_line[q].astype(f32)

time: 40 us -> 42 us (1.050)
  Pallas kernels: 38.2 us -> 40.2 us
    pallas_call x1, Pallas kernels: 38.2 us -> 40.2 us  [local(): pl.pallas_call(functools.partial(step_kernel, n, strips), out_shape=jax.S...]
where the time goes in v4:
time: 42 us; the launch traced here: 41.8 us
  Pallas kernels  40.2 us (96%)
  other arithmetic  1.57 us (4%)
    pallas_call x1, Pallas kernels, local(): pl.pallas_call(functools.partial(step_kernel, n, strips), out_shape=jax.S...  40.2 us
    sub x1, other arithmetic, local(): return model - step_size * gradient  1.57 us

profile of v4, /device:TPU:0, one launch (start us, length us, event | category | flops | bytes accessed | tf_op | source)
XLA Modules:
  0.0 41.8 jit_solution(9236560275049198247)
XLA Ops:
  0.0 0.0 copy-start
  0.0 40.2 %shard_map.73 = f32[256,128]{1,0:T(8,128)} custom-call(f32[256,128]{1,0:T(8,128)} %model_ref.1, s32[4,16]{1,0:T(4,128)} %bitcast.3, s32[16]{0:T(128)} %psf_index.1, f32[16]{0:T(128)} %weights.1, bf16[8,4,25]{2,1,0:T(4,128)(2,1)} %psf_rows.1, bf16[8,4,25]{2,1,0:T(4,128)(2,1)} %psf_cols.1, bf16[256,2048]{1,0:T(8,128)(2,1)} %bitcast.2), custom_call_target="tpu_custom_call" | custom-call | tf_op jit(solution)/shard_map/pallas_call | solution.py:331
  40.2 0.0 copy-done
  40.3 1.6 %multiply_subtract_fusion = f32[256,128]{1,0:T(8,128)} fusion(f32[256,128]{1,0:T(8,128)S(1)} %copy-done, f32[256,128]{1,0:T(8,128)} %shard_map.73), kind=kLoop, calls=%fused_computation | loop fusion | flops 65536 | bytes 393216 | tf_op jit(solution)/shard_map/sub | solution.py:357
Async XLA Ops:
  0.0 40.2 %copy-start = (f32[256,128]{1,0:T(8,128)S(1)}, f32[256,128]{1,0:T(8,128)}, u32[]{:S(2)}) copy-start(f32[256,128]{1,0:T(8,128)} %model_ref.1) | copy-start | bytes 393220
